TPU v7x, 512 devices: a whole 4x8x8 slice. The times are simulated.
512 devices in a mesh: dp: 64 (over y, x, core), tensor: 8 (over z).
Axes of the slice: x: 4, y: 8, z: 8, core: 2. Of those that a mesh axis runs over, the one named last changes fastest.
Arguments:
- hidden_act: bfloat16 [32768, 1408], P('dp', 'tensor'), may hold values from -6 to 6
- cotangent: bfloat16 [32768, 2048], P('dp', 'tensor'), may hold values from -4 to 4
- down_table: bfloat16 [1408, 64, 2048], P('tensor', 'dp'), may hold values from -0.15625 to 0.15625
- expert_ids: int32 [128, 4], P('dp'), may hold values from 0 to 31, as said below
- merge_weights: float32 [128, 4], P('dp'), may hold values from 0.1 to 1
- owner_slot: int32 [32], replicated, may hold values from 0 to 63, as said below
Outputs:
- layer_out: bfloat16 [32768, 2048], P('dp', 'tensor')
- grad_hidden: bfloat16 [32768, 1408], P('dp', 'tensor')
- expert_grad: float32 [1408, 64, 2048], P('tensor', 'dp')
Inputs may be any that keep to these rules, and one draw needn't show every extreme that they name: `expert_ids`: each segment lists 4 different experts; the 2 segments of one index of dp list exactly 6 different experts together. `owner_slot`: different experts have different slots; slot 63 always holds an expert.
All inputs are finite; a program needn't handle non-finite values.
Results may differ from a plain program's by a relative error of at most 0.013.
Values may be sent and summed in bfloat16 or wider, within the bound.
A program may use at most 128 MiB of HBM per device.

v0:
```python
import jax
import jax.numpy as jnp
from jax import lax
from jax.sharding import PartitionSpec as P

E = 32
K = 4
POOL = 6


def pool_members(id_rows):
    listed = id_rows.reshape(-1)
    experts = jnp.arange(E, dtype=jnp.int32)
    present = jnp.any(listed[None, :] == experts[:, None], axis=1)
    ranking = jnp.cumsum(present.astype(jnp.int32)) - 1
    places = jnp.arange(POOL, dtype=jnp.int32)
    chosen = present[None, :] & (ranking[None, :] == places[:, None])
    return jnp.sum(jnp.where(chosen, experts[None, :], 0), axis=1)


def merge_coefficients(id_rows, weight_rows, targets):
    matches = id_rows[:, :, None] == targets[None, None, :]
    return jnp.sum(jnp.where(matches, weight_rows[:, :, None], 0.0), axis=1)


def body(hidden_act, cotangent, down_table, expert_ids, merge_weights, owner_slot):
    dp_count = lax.axis_size("dp")
    seg_count = expert_ids.shape[0]
    ff_local, slot_local, width = down_table.shape
    stripe = width // dp_count
    row_count = hidden_act.shape[0]
    seg_len = row_count // seg_count
    every_expert = jnp.arange(E, dtype=jnp.int32)
    all_ids, all_weights = (
        lax.all_gather(expert_ids, "dp", axis=0, tiled=True),
        lax.all_gather(merge_weights, "dp", axis=0, tiled=True),
    )
    ids_by_dev = all_ids.reshape(dp_count, seg_count, K)
    weights_by_dev = all_weights.reshape(dp_count, seg_count, K)
    pools_all = jax.vmap(pool_members)(ids_by_dev)
    my_pool = pools_all[lax.axis_index("dp")]
    my_coef = merge_coefficients(expert_ids, merge_weights, my_pool)
    member_table = (pools_all.T[:, :, None] == every_expert[None, None, :]).astype(jnp.bfloat16)
    stripes = lax.all_to_all(down_table, "dp", split_axis=2, concat_axis=1, tiled=True)
    by_expert = jnp.take(stripes, owner_slot, axis=1)
    outgoing = jnp.take(by_expert, pools_all.T, axis=1).reshape(ff_local, POOL, width)
    panel_set = lax.all_to_all(outgoing, "dp", split_axis=2, concat_axis=2, tiled=True)
    merged = jnp.sum(
        panel_set[:, None, :, :].astype(jnp.float32) * my_coef[None, :, :, None], axis=2
    ).astype(jnp.bfloat16)
    hidden_seg = hidden_act.reshape(seg_count, seg_len, ff_local)
    partial_rows = jnp.einsum(
        "stf,fsd->std", hidden_seg, merged, preferred_element_type=jnp.float32
    ).reshape(row_count, width)
    layer_out = lax.psum_scatter(
        partial_rows.astype(jnp.bfloat16), "tensor", scatter_dimension=1, tiled=True
    )
    full_cot = lax.all_gather(cotangent, "tensor", axis=1, tiled=True)
    cot_seg = full_cot.reshape(seg_count, seg_len, width)
    grad_hidden = (
        jnp.einsum("std,fsd->stf", cot_seg, merged, preferred_element_type=jnp.float32)
        .astype(jnp.bfloat16)
        .reshape(row_count, ff_local)
    )
    seg_grads = jnp.einsum(
        "stf,std->fsd", hidden_seg, cot_seg, preferred_element_type=jnp.float32
    ).astype(jnp.bfloat16)
    returned = lax.all_to_all(seg_grads, "dp", split_axis=2, concat_axis=2, tiled=True).reshape(
        ff_local, seg_count, dp_count, stripe
    )
    pool_coef = jax.vmap(merge_coefficients)(ids_by_dev, weights_by_dev, pools_all)
    coef_view = jnp.transpose(pool_coef, (1, 2, 0))
    group_sums = jnp.sum(
        returned[:, :, None, :, :].astype(jnp.float32) * coef_view[None, :, :, :, None], axis=1
    ).astype(jnp.bfloat16)
    grad_stripes = jnp.einsum(
        "fprd,pre->fed", group_sums, member_table, preferred_element_type=jnp.float32
    )
    slotted = (
        jnp.zeros((ff_local, slot_local * dp_count, stripe), jnp.float32)
        .at[:, owner_slot, :]
        .set(grad_stripes)
    )
    expert_grad = lax.all_to_all(
        slotted.astype(jnp.bfloat16), "dp", split_axis=1, concat_axis=2, tiled=True
    ).astype(slotted.dtype)
    return (layer_out, grad_hidden, expert_grad)


def solution(mesh):
    placed = (
        P("dp", "tensor"),
        P("dp", "tensor"),
        P("tensor", "dp", None),
        P("dp", None),
        P("dp", None),
        P(),
    )
    return jax.shard_map(
        body,
        mesh=mesh,
        in_specs=placed,
        out_specs=(P("dp", "tensor"), P("dp", "tensor"), P("tensor", "dp", None)),
        check_vma=False,
    )
```

profile of v0, /device:TPU:1, one launch (start us, length us, event | category | flops | bytes accessed | tf_op | source)
XLA Modules:
  0.0 478.6 jit_solution(9711148216334973201)
XLA Ops:
  7.2 4.5 copy.81
  12.2 11.6 %reduce.2 = bf16[2048,176]{1,0:T(8,128)(2,1)S(1)} reduce(bf16[2048,1,176]{2,1,0:T(2,128)(2,1)S(1)} %bitcast.55, bf16[]{:T(256)} %broadcast.42), dimensions={1}, to_apply=%bitcast.44.reduce_sub_computation | reduce | bytes 1441794
  23.9 2.6 reshape.124
  26.5 11.6 %all-to-all-start = ((bf16[64,2,2816]{2,1,0:T(2,128)(2,1)}), bf16[64,2,2816]{2,1,0:T(2,128)(2,1)S(1)}, u32[]{:S(2)}, u32[]{:S(2)}) async-start(bf16[64,2,2816]{2,1,0:T(2,128)(2,1)} %reshape.124), calls=%async_computation | async-start | bytes 1441792 | tf_op jit(solution)/shard_map/all_to_all | solution.py:44
  38.1 50.6 %all-gather = s32[64,2,4]{2,1,0:T(2,128)S(1)} all-gather(s32[1,2,4]{2,1,0:T(2,128)S(1)} %bitcast.65), channel_id=1, replica_groups=mesh['dp'=64,'tensor'=8] {'dp'}, dimensions={0}, use_global_device_ids=true | all-gather | bytes 2080 | tf_op jit(solution)/shard_map/all_gather | solution.py:35
  89.8 3.2 reshape.125
  93.8 13.3 %gather_fusion.1 = bf16[384,176,32]{1,2,0:T(8,128)(2,1)} fusion(bf16[176,32,32]{0,2,1:T(8,128)(2,1)S(1)} %select_bitcast_fusion, s32[1024]{0:T(1024)S(1)} %pad_clamp_fusion), kind=kCustom, calls=%fused_computation.1 | custom fusion | bytes 8652288 | tf_op jit(solution)/shard_map/jit(_take)/gather | solution.py:46
  107.2 6.2 %broadcast_select_fusion = bf16[176,6,2048]{0,2,1:T(8,128)(2,1)S(1)} fusion(bf16[176,6,2048]{0,2,1:T(8,128)(2,1)} %bitcast.51, pred[6,2048]{1,0:T(8,128)(4,1)S(1)} %broadcast_in_dim.86), kind=kLoop, calls=%fused_computation.7 | loop fusion | flops 2162688 | bytes 8663040 | tf_op jit(solution)/shard_map/jit(_take)/select_n | solution.py:46
  113.4 22.3 %copy.82 = bf16[176,6,2048]{0,1,2:T(8,128)(2,1)} copy(bf16[176,6,2048]{0,2,1:T(8,128)(2,1)S(1)} %broadcast_select_fusion) | data formatting | bytes 8650752 | tf_op jit(solution)/shard_map/jit(_take)/select_n | solution.py:46
  135.7 8.6 %all-to-all-start.1 = ((bf16[176,6,2048]{0,1,2:T(8,128)(2,1)}), bf16[176,6,2048]{0,1,2:T(8,128)(2,1)}, u32[]{:S(2)}, u32[]{:S(2)}) async-start(bf16[176,6,2048]{0,1,2:T(8,128)(2,1)} %copy.82), calls=%async_computation.1 | async-start | bytes 16777216 | tf_op jit(solution)/shard_map/all_to_all | solution.py:47
  145.1 53.0 %all-gather.4.cloned.1.call-done = bf16[512,2048]{1,0:T(8,128)(2,1)} async-done(((bf16[512,256]{1,0:T(8,128)(2,1)}), bf16[512,2048]{1,0:T(8,128)(2,1)}) %all-gather.4.cloned.1.call-update) | async-done | bytes 2097168 | tf_op jit(solution)/shard_map/all_gather | solution.py:58
  198.0 2.1 fusion.2
  200.2 3.8 copy.87
  204.0 122.7 %all-to-all-done.1 = bf16[176,6,2048]{0,1,2:T(8,128)(2,1)} async-done(((bf16[176,6,2048]{0,1,2:T(8,128)(2,1)}), bf16[176,6,2048]{0,1,2:T(8,128)(2,1)}, u32[]{:S(2)}, u32[]{:S(2)}) %all-to-all-start.1) | async-done | bytes 4325408 | tf_op jit(solution)/shard_map/all_to_all | solution.py:47
  326.7 10.1 %all-to-all-start.2 = ((bf16[176,2,2048]{0,1,2:T(2,128)(2,1)}), bf16[176,2,2048]{0,1,2:T(2,128)(2,1)S(1)}, u32[]{:S(2)}, u32[]{:S(2)}) async-start(bf16[176,2,2048]{0,1,2:T(2,128)(2,1)} %copy.87), calls=%async_computation.3 | async-start | bytes 4194304 | tf_op jit(solution)/shard_map/all_to_all | solution.py:68
  337.1 11.3 %copy.83 = bf16[176,6,2048]{2,0,1:T(8,128)(2,1)} copy(bf16[176,6,2048]{0,1,2:T(8,128)(2,1)} %all-to-all-done.1) | data formatting | bytes 8650752 | tf_op jit(solution)/shard_map/all_to_all | solution.py:47
  348.4 6.6 %convert_element_type.68 = f32[176,6,2048]{2,0,1:T(8,128)} convert(bf16[176,6,2048]{2,0,1:T(8,128)(2,1)} %copy.83) | non-fusion elementwise | flops 2162688 | bytes 12976128 | tf_op jit(solution)/shard_map/convert_element_type | solution.py:49
  355.0 4.8 multiply_reduce_fusion.1
  360.9 2.1 convolution_convert_fusion
  363.0 53.9 %all-gather.1 = f32[64,2,4]{2,1,0:T(2,128)S(1)} all-gather(f32[1,2,4]{2,1,0:T(2,128)S(1)} %bitcast.66), channel_id=1, replica_groups=mesh['dp'=64,'tensor'=8] {'dp'}, dimensions={0}, use_global_device_ids=true | all-gather | bytes 2080 | tf_op jit(solution)/shard_map/all_gather | solution.py:36
  417.7 4.2 multiply_reduce_fusion
  421.9 3.7 fusion.3
  428.2 35.5 %all_to_all.31 = bf16[176,64,32]{0,2,1:T(8,128)(2,1)S(1)} all-to-all(bf16[176,64,32]{0,2,1:T(8,128)(2,1)S(1)} %convert_element_type.80), channel_id=1, replica_groups=mesh['dp'=64,'tensor'=8] {'dp'}, dimensions={1} | all-to-all | bytes 1441792 | tf_op jit(solution)/shard_map/all_to_all | solution.py:84
  465.2 5.1 %copy.93 = f32[176,1,2048]{2,1,0:T(1,128)} copy(f32[176,1,2048]{0,2,1:T(8,128)} %bitcast_convert_fusion) | data formatting | bytes 2883584
  (54 shorter events, 10.8 us)
Async XLA Ops:
  23.9 14.3 %copy-start.4 = (s32[2,4]{1,0:T(2,128)S(1)}, s32[2,4]{1,0:T(2,128)}, u32[]{:S(2)}) copy-start(s32[2,4]{1,0:T(2,128)} %param.9) | copy-start | bytes 100
  23.9 65.9 %copy-start.6 = (s32[32]{0:T(128)S(1)}, s32[32]{0:T(128)}, u32[]{:S(2)}) copy-start(s32[32]{0:T(128)} %param.11) | copy-start | bytes 388
  26.5 63.3 %all-to-all-start = ((bf16[64,2,2816]{2,1,0:T(2,128)(2,1)}), bf16[64,2,2816]{2,1,0:T(2,128)(2,1)S(1)}, u32[]{:S(2)}, u32[]{:S(2)}) async-start(bf16[64,2,2816]{2,1,0:T(2,128)(2,1)} %reshape.124), calls=%async_computation | async-start | bytes 1441792 | tf_op jit(solution)/shard_map/all_to_all | solution.py:44
  135.7 62.3 %copy-start.3 = (bf16[512,176]{0,1:T(8,128)(2,1)S(1)}, bf16[512,176]{0,1:T(8,128)(2,1)}, u32[]{:S(2)}) copy-start(bf16[512,176]{0,1:T(8,128)(2,1)} %param.6) | copy-start | bytes 540676
  135.7 191.0 %all-to-all-start.1 = ((bf16[176,6,2048]{0,1,2:T(8,128)(2,1)}), bf16[176,6,2048]{0,1,2:T(8,128)(2,1)}, u32[]{:S(2)}, u32[]{:S(2)}) async-start(bf16[176,6,2048]{0,1,2:T(8,128)(2,1)} %copy.82), calls=%async_computation.1 | async-start | bytes 16777216 | tf_op jit(solution)/shard_map/all_to_all | solution.py:47
  144.3 53.7 %all-gather.4.cloned.1.call-start = ((), (), s32[]{:S(2)}) async-start(), calls=%async_computation.6 | async-start | bytes 2359296 | tf_op jit(solution)/shard_map/all_gather | solution.py:58
  204.0 133.0 %copy-start.5 = (f32[2,4]{1,0:T(2,128)S(1)}, f32[2,4]{1,0:T(2,128)}, u32[]{:S(2)}) copy-start(f32[2,4]{1,0:T(2,128)} %param.10) | copy-start | bytes 100
  326.7 90.3 %all-to-all-start.2 = ((bf16[176,2,2048]{0,1,2:T(2,128)(2,1)}), bf16[176,2,2048]{0,1,2:T(2,128)(2,1)S(1)}, u32[]{:S(2)}, u32[]{:S(2)}) async-start(bf16[176,2,2048]{0,1,2:T(2,128)(2,1)} %copy.87), calls=%async_computation.3 | async-start | bytes 4194304 | tf_op jit(solution)/shard_map/all_to_all | solution.py:68
  336.8 135.0 %reduce-scatter.2.cloned.1.call-start = ((), (), s32[]{:S(2)}) async-start(), calls=%async_computation.5 | async-start | bytes 2359296 | tf_op jit(solution)/shard_map/reduce_scatter | solution.py:55
  359.8 1.1 copy-start
  465.2 5.1 %copy-start.1 = (bf16[176,2,2048]{2,0,1:T(8,128)(2,1)S(1)}, bf16[176,2,2048]{2,0,1:T(8,128)(2,1)}, u32[]{:S(2)}) copy-start(bf16[176,2,2048]{2,0,1:T(8,128)(2,1)} %copy-done) | copy-start | bytes 4325380
  465.2 5.1 %copy-start.2 = (bf16[512,2048]{1,0:T(8,128)(2,1)S(1)}, bf16[512,2048]{1,0:T(8,128)(2,1)}, u32[]{:S(2)}) copy-start(bf16[512,2048]{1,0:T(8,128)(2,1)} %all-gather.4.cloned.1.call-done) | copy-start | bytes 6291460
Sparse Core Ops, SparseCore 0:
  147.2 50.8 all-gather.3
  363.1 45.3 reduce-scatter.1
where the time goes:
time: 480 us; the launch traced here: 479 us
  waiting for transfers between devices  176 us (37%)
  blocking collectives  140 us (29%)
  local copies, waits for them, and re-layouts  72.6 us (15%)
  other arithmetic  36.2 us (8%)
  starting transfers between devices  30.4 us (6%)
  between operations  14.3 us (3%)
  matrix products  8.77 us (2%)
    all_to_all x1, waiting for transfers between devices, body(): lax.all_to_all(outgoing, 'dp', split_axis=2, concat_axis=2, tiled=True)  123 us
    all_gather x1, blocking collectives, body(): lax.all_gather(merge_weights, 'dp', axis=0, tiled=True)  53.9 us
    all_gather x1, waiting for transfers between devices, body(): full_cot = lax.all_gather(cotangent, 'tensor', axis=1, tiled=True)  53 us
    all_gather x1, blocking collectives, body(): lax.all_gather(expert_ids, 'dp', axis=0, tiled=True)  50.6 us
    all_to_all x1, blocking collectives, body(): lax.all_to_all(slotted.astype(jnp.bfloat16), 'dp', split_axis=1, concat_a...  35.5 us
    select_n x1, local copies, waits for them, and re-layouts, body(): jnp.take(by_expert, pools_all.T, axis=1).reshape(ff_local, POOL, width)  22.3 us
    unnamed x20, local copies, waits for them, and re-layouts  17.2 us
    gather x1, local copies, waits for them, and re-layouts, body(): jnp.take(by_expert, pools_all.T, axis=1).reshape(ff_local, POOL, width)  13.3 us
  transfers between devices with their start and end apart: 5, of which 2 were waited for; matrix products, arithmetic and copies ran while one was open for 11% of the time, Pallas kernels for 0%

commit v1 on v0

--- a/solution.py
+++ b/solution.py
@@ -6,6 +6,16 @@
 E = 32
 K = 4
 POOL = 6
+
+
+def choose_the_screen(incoming_x):
+    n = lax.axis_size("dp")
+    top = range(incoming_x.ndim)
+    mat_out = map(lambda it: n if it == 0 else 1, top)
+    part_next = list(mat_out)
+    passed = jnp.tile(incoming_x, part_next)
+    side_arr = lax.all_to_all(passed, axis_name="dp", split_axis=0, concat_axis=0, tiled=True)
+    return side_arr
 
 
 def pool_members(id_rows):
@@ -32,7 +42,7 @@
     seg_len = row_count // seg_count
     every_expert = jnp.arange(E, dtype=jnp.int32)
     all_ids, all_weights = (
-        lax.all_gather(expert_ids, "dp", axis=0, tiled=True),
+        choose_the_screen(expert_ids),
         lax.all_gather(merge_weights, "dp", axis=0, tiled=True),
     )
     ids_by_dev = all_ids.reshape(dp_count, seg_count, K)

time: 480 us -> 459 us (0.956)
  blocking collectives: 140 us -> 89.4 us
  waiting for transfers between devices: 176 us -> 197 us
  starting transfers between devices: 30.4 us -> 38.4 us
    all_gather x1 -> x0, blocking collectives: 50.6 us -> none  [body(): lax.all_gather(expert_ids, 'dp', axis=0, tiled=True)]
    all_to_all x1, waiting for transfers between devices: 0.01 us -> 20.6 us  [body(): lax.all_to_all(down_table, 'dp', split_axis=2, concat_axis=1, tiled=True)]
    all_to_all x0 -> x1, starting transfers between devices: none -> 11.6 us  [choose_the_screen(): lax.all_to_all(passed, axis_name='dp', split_axis=0, concat_axis=0, tiled...]
  transfers between devices with their start and end apart: 5 -> 6, of which waited for: 2 -> 3; matrix products, arithmetic and copies ran while one was open for 11% -> 15% of each run, Pallas kernels for 0% -> 0%
where the time goes in v1:
time: 459 us; the launch traced here: 458 us
  waiting for transfers between devices  197 us (43%)
  blocking collectives  89.4 us (19%)
  local copies, waits for them, and re-layouts  73.9 us (16%)
  starting transfers between devices  38.4 us (8%)
  other arithmetic  36.2 us (8%)
  between operations  14.3 us (3%)
  matrix products  8.77 us (2%)
    all_to_all x1, waiting for transfers between devices, body(): lax.all_to_all(outgoing, 'dp', split_axis=2, concat_axis=2, tiled=True)  123 us
    all_gather x1, blocking collectives, body(): lax.all_gather(merge_weights, 'dp', axis=0, tiled=True)  53.9 us
    all_gather x1, waiting for transfers between devices, body(): full_cot = lax.all_gather(cotangent, 'tensor', axis=1, tiled=True)  53 us
    all_to_all x1, blocking collectives, body(): lax.all_to_all(slotted.astype(jnp.bfloat16), 'dp', split_axis=1, concat_a...  35.5 us
    select_n x1, local copies, waits for them, and re-layouts, body(): jnp.take(by_expert, pools_all.T, axis=1).reshape(ff_local, POOL, width)  22.3 us
    all_to_all x1, waiting for transfers between devices, body(): lax.all_to_all(down_table, 'dp', split_axis=2, concat_axis=1, tiled=True)  20.6 us
    unnamed x20, local copies, waits for them, and re-layouts  17.2 us
    gather x1, local copies, waits for them, and re-layouts, body(): jnp.take(by_expert, pools_all.T, axis=1).reshape(ff_local, POOL, width)  13.3 us
  transfers between devices with their start and end apart: 6, of which 3 were waited for; matrix products, arithmetic and copies ran while one was open for 15% of the time, Pallas kernels for 0%

profile of v1, /device:TPU:1, one launch (start us, length us, event | category | flops | bytes accessed | tf_op | source)
XLA Modules:
  0.0 457.9 jit_solution(16521613362879931998)
XLA Ops:
  8.5 11.6 %all-to-all-start = ((s32[64,2,4]{2,1,0:T(2,128)}), s32[64,2,4]{2,1,0:T(2,128)S(1)}, u32[]{:S(2)}, u32[]{:S(2)}) async-start(s32[64,2,4]{2,1,0:T(2,128)} %tile.2), calls=%async_computation | async-start | bytes 131072 | tf_op jit(solution)/shard_map/all_to_all | solution.py:17
  20.1 4.5 copy.81
  25.2 11.6 %reduce.2 = bf16[2048,176]{1,0:T(8,128)(2,1)S(1)} reduce(bf16[2048,1,176]{2,1,0:T(2,128)(2,1)S(1)} %bitcast.54, bf16[]{:T(256)} %broadcast.45), dimensions={1}, to_apply=%bitcast.43.reduce_sub_computation | reduce | bytes 1441794
  36.8 2.6 reshape.129
  39.4 10.3 %all-to-all-start.1 = ((bf16[64,2,2816]{2,1,0:T(2,128)(2,1)}), bf16[64,2,2816]{2,1,0:T(2,128)(2,1)S(1)}, u32[]{:S(2)}, u32[]{:S(2)}) async-start(bf16[64,2,2816]{2,1,0:T(2,128)(2,1)} %reshape.129), calls=%async_computation.1 | async-start | bytes 1441792 | tf_op jit(solution)/shard_map/all_to_all | solution.py:54
  50.8 20.6 %all-to-all-done.1 = bf16[64,2,2816]{2,1,0:T(2,128)(2,1)S(1)} async-done(((bf16[64,2,2816]{2,1,0:T(2,128)(2,1)}), bf16[64,2,2816]{2,1,0:T(2,128)(2,1)S(1)}, u32[]{:S(2)}, u32[]{:S(2)}) %all-to-all-start.1) | async-done | bytes 720928 | tf_op jit(solution)/shard_map/all_to_all | solution.py:54
  71.3 3.1 reshape.130
  75.4 13.3 %gather_fusion.1 = bf16[384,176,32]{1,2,0:T(8,128)(2,1)} fusion(bf16[176,32,32]{0,2,1:T(8,128)(2,1)S(1)} %select_bitcast_fusion, s32[1024]{0:T(1024)S(1)} %pad_clamp_fusion), kind=kCustom, calls=%fused_computation.1 | custom fusion | bytes 8652288 | tf_op jit(solution)/shard_map/jit(_take)/gather | solution.py:56
  88.7 6.2 %broadcast_select_fusion = bf16[176,6,2048]{0,2,1:T(8,128)(2,1)S(1)} fusion(bf16[176,6,2048]{0,2,1:T(8,128)(2,1)} %bitcast.50, pred[6,2048]{1,0:T(8,128)(4,1)S(1)} %broadcast_in_dim.86), kind=kLoop, calls=%fused_computation.7 | loop fusion | flops 2162688 | bytes 8663040 | tf_op jit(solution)/shard_map/jit(_take)/select_n | solution.py:56
  94.9 22.3 %copy.82 = bf16[176,6,2048]{0,1,2:T(8,128)(2,1)} copy(bf16[176,6,2048]{0,2,1:T(8,128)(2,1)S(1)} %broadcast_select_fusion) | data formatting | bytes 8650752 | tf_op jit(solution)/shard_map/jit(_take)/select_n | solution.py:56
  117.2 6.3 %all-to-all-start.2 = ((bf16[176,6,2048]{0,1,2:T(8,128)(2,1)}), bf16[176,6,2048]{0,1,2:T(8,128)(2,1)}, u32[]{:S(2)}, u32[]{:S(2)}) async-start(bf16[176,6,2048]{0,1,2:T(8,128)(2,1)} %copy.82), calls=%async_computation.2 | async-start | bytes 16777216 | tf_op jit(solution)/shard_map/all_to_all | solution.py:57
  124.3 53.0 %all-gather.3.cloned.1.call-done = bf16[512,2048]{1,0:T(8,128)(2,1)} async-done(((bf16[512,256]{1,0:T(8,128)(2,1)}), bf16[512,2048]{1,0:T(8,128)(2,1)}) %all-gather.3.cloned.1.call-update) | async-done | bytes 2097168 | tf_op jit(solution)/shard_map/all_gather | solution.py:68
  177.3 2.1 fusion.2
  179.4 3.8 copy.87
  183.3 122.7 %all-to-all-done.2 = bf16[176,6,2048]{0,1,2:T(8,128)(2,1)} async-done(((bf16[176,6,2048]{0,1,2:T(8,128)(2,1)}), bf16[176,6,2048]{0,1,2:T(8,128)(2,1)}, u32[]{:S(2)}, u32[]{:S(2)}) %all-to-all-start.2) | async-done | bytes 4325408 | tf_op jit(solution)/shard_map/all_to_all | solution.py:57
  306.0 10.1 %all-to-all-start.3 = ((bf16[176,2,2048]{0,1,2:T(2,128)(2,1)}), bf16[176,2,2048]{0,1,2:T(2,128)(2,1)S(1)}, u32[]{:S(2)}, u32[]{:S(2)}) async-start(bf16[176,2,2048]{0,1,2:T(2,128)(2,1)} %copy.87), calls=%async_computation.4 | async-start | bytes 4194304 | tf_op jit(solution)/shard_map/all_to_all | solution.py:78
  316.4 11.3 %copy.83 = bf16[176,6,2048]{2,0,1:T(8,128)(2,1)} copy(bf16[176,6,2048]{0,1,2:T(8,128)(2,1)} %all-to-all-done.2) | data formatting | bytes 8650752 | tf_op jit(solution)/shard_map/all_to_all | solution.py:57
  327.7 6.6 %convert_element_type.68 = f32[176,6,2048]{2,0,1:T(8,128)} convert(bf16[176,6,2048]{2,0,1:T(8,128)(2,1)} %copy.83) | non-fusion elementwise | flops 2162688 | bytes 12976128 | tf_op jit(solution)/shard_map/convert_element_type | solution.py:59
  334.3 4.8 %multiply_reduce_fusion.1 = bf16[176,2,2048]{2,0,1:T(8,128)(2,1)S(1)} fusion(f32[2,6]{1,0:T(2,128)S(1)} %select_reduce_fusion.2, f32[176,6,2048]{2,0,1:T(8,128)} %convert_element_type.68), kind=kLoop, calls=%fused_computation.4 | loop fusion | flops 7929856 | bytes 10092592 | tf_op jit(solution)/shard_map/reduce_sum | solution.py:58
  342.3 53.9 %all-gather = f32[64,2,4]{2,1,0:T(2,128)S(1)} all-gather(f32[1,2,4]{2,1,0:T(2,128)S(1)} %bitcast.64), channel_id=1, replica_groups=mesh['dp'=64,'tensor'=8] {'dp'}, dimensions={0}, use_global_device_ids=true | all-gather | bytes 2080 | tf_op jit(solution)/shard_map/all_gather | solution.py:46
  396.9 4.2 multiply_reduce_fusion
  401.2 3.7 fusion.3
  407.5 35.5 %all_to_all.37 = bf16[176,64,32]{0,2,1:T(8,128)(2,1)S(1)} all-to-all(bf16[176,64,32]{0,2,1:T(8,128)(2,1)S(1)} %convert_element_type.80), channel_id=1, replica_groups=mesh['dp'=64,'tensor'=8] {'dp'}, dimensions={1} | all-to-all | bytes 1441792 | tf_op jit(solution)/shard_map/all_to_all | solution.py:94
  444.4 5.1 %copy.93 = f32[176,1,2048]{2,1,0:T(1,128)} copy(f32[176,1,2048]{0,2,1:T(8,128)} %bitcast_convert_fusion) | data formatting | bytes 2883584
  (56 shorter events, 14.3 us)
Async XLA Ops:
  8.5 30.9 %all-to-all-start = ((s32[64,2,4]{2,1,0:T(2,128)}), s32[64,2,4]{2,1,0:T(2,128)S(1)}, u32[]{:S(2)}, u32[]{:S(2)}) async-start(s32[64,2,4]{2,1,0:T(2,128)} %tile.2), calls=%async_computation | async-start | bytes 131072 | tf_op jit(solution)/shard_map/all_to_all | solution.py:17
  36.8 12.9 %copy-start.6 = (s32[32]{0:T(128)S(1)}, s32[32]{0:T(128)}, u32[]{:S(2)}) copy-start(s32[32]{0:T(128)} %param.11) | copy-start | bytes 388
  39.4 31.9 %all-to-all-start.1 = ((bf16[64,2,2816]{2,1,0:T(2,128)(2,1)}), bf16[64,2,2816]{2,1,0:T(2,128)(2,1)S(1)}, u32[]{:S(2)}, u32[]{:S(2)}) async-start(bf16[64,2,2816]{2,1,0:T(2,128)(2,1)} %reshape.129), calls=%async_computation.1 | async-start | bytes 1441792 | tf_op jit(solution)/shard_map/all_to_all | solution.py:54
  117.2 60.0 %copy-start.3 = (bf16[512,176]{0,1:T(8,128)(2,1)S(1)}, bf16[512,176]{0,1:T(8,128)(2,1)}, u32[]{:S(2)}) copy-start(bf16[512,176]{0,1:T(8,128)(2,1)} %param.6) | copy-start | bytes 540676
  117.2 188.7 %all-to-all-start.2 = ((bf16[176,6,2048]{0,1,2:T(8,128)(2,1)}), bf16[176,6,2048]{0,1,2:T(8,128)(2,1)}, u32[]{:S(2)}, u32[]{:S(2)}) async-start(bf16[176,6,2048]{0,1,2:T(8,128)(2,1)} %copy.82), calls=%async_computation.2 | async-start | bytes 16777216 | tf_op jit(solution)/shard_map/all_to_all | solution.py:57
  123.6 53.7 %all-gather.3.cloned.1.call-start = ((), (), s32[]{:S(2)}) async-start(), calls=%async_computation.7 | async-start | bytes 2359296 | tf_op jit(solution)/shard_map/all_gather | solution.py:68
  183.3 133.0 %copy-start.4 = (s32[2,4]{1,0:T(2,128)S(1)}, s32[2,4]{1,0:T(2,128)}, u32[]{:S(2)}) copy-start(s32[2,4]{1,0:T(2,128)} %param.9) | copy-start | bytes 100
  183.3 133.0 %copy-start.5 = (f32[2,4]{1,0:T(2,128)S(1)}, f32[2,4]{1,0:T(2,128)}, u32[]{:S(2)}) copy-start(f32[2,4]{1,0:T(2,128)} %param.10) | copy-start | bytes 100
  306.0 90.3 %all-to-all-start.3 = ((bf16[176,2,2048]{0,1,2:T(2,128)(2,1)}), bf16[176,2,2048]{0,1,2:T(2,128)(2,1)S(1)}, u32[]{:S(2)}, u32[]{:S(2)}) async-start(bf16[176,2,2048]{0,1,2:T(2,128)(2,1)} %copy.87), calls=%async_computation.4 | async-start | bytes 4194304 | tf_op jit(solution)/shard_map/all_to_all | solution.py:78
  316.0 135.0 %reduce-scatter.2.cloned.1.call-start = ((), (), s32[]{:S(2)}) async-start(), calls=%async_computation.6 | async-start | bytes 2359296 | tf_op jit(solution)/shard_map/reduce_scatter | solution.py:65
  339.1 1.1 copy-start
  444.4 5.1 %copy-start.1 = (bf16[176,2,2048]{2,0,1:T(8,128)(2,1)S(1)}, bf16[176,2,2048]{2,0,1:T(8,128)(2,1)}, u32[]{:S(2)}) copy-start(bf16[176,2,2048]{2,0,1:T(8,128)(2,1)} %copy-done) | copy-start | bytes 4325380
  444.4 5.1 %copy-start.2 = (bf16[512,2048]{1,0:T(8,128)(2,1)S(1)}, bf16[512,2048]{1,0:T(8,128)(2,1)}, u32[]{:S(2)}) copy-start(bf16[512,2048]{1,0:T(8,128)(2,1)} %all-gather.3.cloned.1.call-done) | copy-start | bytes 6291460
Sparse Core Ops, SparseCore 0:
  126.4 50.8 all-gather.2
  342.4 45.3 reduce-scatter.1
